TPU v7x, 256 devices: a whole 4x4x8 slice. The times are simulated.
256 devices in a mesh: dp: 16 (over y_lo, x, core), chan: 16 (over y_hi, z).
Axes of the slice: x: 4, y: 4 (y_hi: 2, y_lo: 2; y = y_hi * 2 + y_lo), z: 8, core: 2. Of those that a mesh axis runs over, the one named last changes fastest.
Arguments:
- anchors: bfloat16 [256, 128, 4096], P('dp', 'chan'), may hold values from -15 to 15
- views: bfloat16 [256, 128, 4096], P('dp', 'chan'), may hold values from -15 to 15
- dw_weight: float32 [128, 4], replicated, may hold values from -3 to 3
- pw_weight: bfloat16 [256, 128], replicated, may hold values from -0.5 to 0.5
- proj_weight: bfloat16 [256, 1024], replicated, may hold values from -0.375 to 0.375
- partner: int32 [256], P('dp'), may hold values from 0 to 255, each once
Outputs:
- loss: float32 [256], P('dp')
- grad_dw: float32 [128, 4], P('chan')
- grad_pw: float32 [256, 128], replicated
- grad_proj: float32 [256, 1024], P('chan', 'dp')
Inputs may be any that keep to these rules, and one draw needn't show every extreme that they name: `partner`: each view index appears exactly once.
All inputs are finite; a program needn't handle non-finite values.
Results may differ from a plain program's by a relative error of at most 0.0044.
Values may be sent and summed in bfloat16 or wider, within the bound.
No kernel may reach another device: no remote copies, remote signals or barrier semaphores. Data moves between devices by JAX's collectives and lax.ppermute only.
A program may use at most 192 MiB of HBM per device.

v0:
```python
import jax
import jax.numpy as jnp
from jax import lax
from jax.sharding import PartitionSpec as P

TAPS = 4
TAP_SPACING = 16
logit_scale = 16.0


def passed_along(value, axis, steps):
    count = lax.axis_size(axis)
    pairs = [(source, (source + steps) % count) for source in range(count)]
    return lax.ppermute(value, axis, pairs)


def depthwise(trace_block, dw_weight):
    widened = trace_block.astype(jnp.float32)
    length = trace_block.shape[2]
    running = jnp.zeros(widened.shape, jnp.float32)
    for tap_index in range(TAPS):
        offset_steps = tap_index * TAP_SPACING
        shifted = jnp.pad(
            widened[:, :, : length - offset_steps], ((0, 0), (0, 0), (offset_steps, 0))
        )
        running = running + dw_weight[None, :, tap_index, None] * shifted
    return running.astype(jnp.bfloat16)


def silu_slope(mixed):
    sigma = jax.nn.sigmoid(mixed)
    return sigma * (1.0 + mixed * (1.0 - sigma))


def kernel_terms(grad_conv, extended):
    rim_width = (TAPS - 1) * TAP_SPACING
    span_width = grad_conv.shape[2]
    columns = []
    for tap_index in range(TAPS):
        begin = rim_width - tap_index * TAP_SPACING
        window = extended[:, :, begin : begin + span_width]
        columns.append(
            jnp.einsum("nct,nct->c", grad_conv, window, preferred_element_type=jnp.float32)
        )
    return jnp.stack(columns, 1)


def block_scores(queries, key_rows, owner_index, partner, factor):
    logits = factor * lax.dot_general(
        queries, key_rows, (((1,), (1,)), ((), ())), preferred_element_type=jnp.float32
    )
    columns = owner_index * key_rows.shape[0] + jnp.arange(key_rows.shape[0], dtype=jnp.int32)
    matches = columns[None, :] == partner[:, None]
    return (logits, matches)


def body(anchors, views, dw_weight, pw_weight, proj_weight, partner):
    stacked = jnp.concatenate([anchors, views], 0)
    pair_count = anchors.shape[0]
    length = anchors.shape[2]
    chan_index = lax.axis_index("chan")
    chan_count = lax.axis_size("chan")
    cycle_index = lax.axis_index("dp")
    cycle_size = lax.axis_size("dp")
    rim_width = (TAPS - 1) * TAP_SPACING
    local_metrics = anchors.shape[1]
    local_kernel = lax.dynamic_slice_in_dim(dw_weight, chan_index * local_metrics, local_metrics, 0)
    conv_local = depthwise(stacked, local_kernel)
    conv_rows = lax.all_to_all(conv_local, "chan", split_axis=2, concat_axis=1, tiled=True)
    mixed = jnp.einsum("fc,nct->nft", pw_weight, conv_rows, preferred_element_type=jnp.float32)
    partial_pool = jnp.sum(jax.nn.silu(mixed), 2) / length
    conv_time, mixed, partial_pool = (conv_rows, mixed, partial_pool)
    pooled = lax.psum(partial_pool, "chan")
    pooled_bf = pooled.astype(jnp.bfloat16)
    embedding = jnp.dot(pooled_bf, proj_weight, preferred_element_type=jnp.float32)
    inverse = lax.rsqrt(jnp.mean(embedding * embedding, 1, keepdims=True) + 1e-06)
    unit_rows = embedding * inverse
    unit_bf = unit_rows.astype(jnp.bfloat16)
    queries = unit_bf[:pair_count]
    own_keys = unit_bf[pair_count:]
    factor = logit_scale / proj_weight.shape[1]

    def total_terms(key_rows, owner_index, totals, positive):
        logits, matches = block_scores(queries, key_rows, owner_index, partner, factor)
        totals = totals + jnp.sum(jnp.exp(logits - logit_scale), 1)
        positive = positive + jnp.sum(jnp.where(matches, logits, 0.0), 1)
        return (totals, positive)

    def first_turn(turn_index, loop_state):
        key_rows, totals, positive = loop_state
        owner_index = (cycle_index - turn_index) % cycle_size
        totals, positive = total_terms(key_rows, owner_index, totals, positive)
        key_rows = passed_along(key_rows, "dp", 1)
        return (key_rows, totals, positive)

    start_zero = jnp.zeros((pair_count,), jnp.float32)
    key_rows, totals, positive = lax.fori_loop(
        0, cycle_size - 1, first_turn, (own_keys, start_zero, start_zero)
    )
    totals, positive = total_terms(
        key_rows, (cycle_index - (cycle_size - 1)) % cycle_size, totals, positive
    )

    def grad_terms(key_rows, owner_index, carried, grad_query):
        logits, matches = block_scores(queries, key_rows, owner_index, partner, factor)
        coeffs = (
            jnp.exp(logits - logit_scale) / totals[:, None] - matches.astype(jnp.float32)
        ).astype(jnp.bfloat16)
        grad_query = grad_query + factor * jnp.dot(
            coeffs, key_rows, preferred_element_type=jnp.float32
        )
        carried = carried + factor * lax.dot_general(
            coeffs, queries, (((0,), (0,)), ((), ())), preferred_element_type=jnp.float32
        )
        return (carried, grad_query)

    def second_turn(turn_index, loop_state):
        key_rows, carried, grad_query = loop_state
        owner_index = (cycle_index - turn_index) % cycle_size
        carried, grad_query = grad_terms(key_rows, owner_index, carried, grad_query)
        key_rows = passed_along(key_rows, "dp", 1)
        carried = passed_along(carried, "dp", 1)
        return (key_rows, carried, grad_query)

    start_grads = jnp.zeros(own_keys.shape, jnp.float32)
    key_rows, carried, grad_query = lax.fori_loop(
        0, cycle_size - 1, second_turn, (own_keys, start_grads, start_grads)
    )
    carried, grad_query = grad_terms(
        key_rows, (cycle_index - (cycle_size - 1)) % cycle_size, carried, grad_query
    )
    grad_key = passed_along(carried, "dp", 1)
    losses = logit_scale + jnp.log(totals) - positive
    grad_unit = jnp.concatenate([grad_query, grad_key], 0)
    grad_embed = inverse * (
        grad_unit - unit_rows * jnp.mean(unit_rows * grad_unit, 1, keepdims=True)
    )
    grad_embed_bf = grad_embed.astype(jnp.bfloat16)
    filter_rows = proj_weight.shape[0] // chan_count
    pooled_rows = lax.dynamic_slice_in_dim(pooled_bf, chan_index * filter_rows, filter_rows, 1)
    proj_terms = lax.dot_general(
        pooled_rows, grad_embed_bf, (((0,), (0,)), ((), ())), preferred_element_type=jnp.float32
    )
    grad_proj = lax.psum_scatter(proj_terms, "dp", scatter_dimension=1, tiled=True)
    grad_pool = lax.dot_general(
        grad_embed_bf, proj_weight, (((1,), (1,)), ((), ())), preferred_element_type=jnp.float32
    )
    grad_mixed = (grad_pool[:, :, None] / length * silu_slope(mixed)).astype(jnp.bfloat16)
    mix_terms = jnp.einsum("nft,nct->fc", grad_mixed, conv_time, preferred_element_type=jnp.float32)
    grad_conv = jnp.einsum(
        "fc,nft->nct", pw_weight, grad_mixed, preferred_element_type=jnp.float32
    ).astype(jnp.bfloat16)
    grad_pw = lax.psum(mix_terms, ("dp", "chan"))
    grad_local = lax.all_to_all(grad_conv, "chan", split_axis=1, concat_axis=2, tiled=True)
    extended = jnp.pad(stacked, ((0, 0), (0, 0), (rim_width, 0)))
    kernel_part = kernel_terms(grad_local, extended)
    grad_dw = lax.psum(kernel_part, "dp")
    return (losses, grad_dw, grad_pw, grad_proj)


def solution(mesh):
    placed = (P("dp", "chan", None), P("dp", "chan", None), P(), P(), P(), P("dp"))
    return jax.shard_map(
        body,
        mesh=mesh,
        in_specs=placed,
        out_specs=(P("dp"), P("chan", None), P(), P("chan", "dp")),
        check_vma=False,
    )
```

profile of v0, /device:TPU:2, one launch (start us, length us, event | category | flops | bytes accessed | tf_op | source)
XLA Modules:
  0.0 708.4 jit_solution(9025586352325555345)
XLA Ops:
  10.7 7.9 %copy.34 = bf16[32,8,4096]{0,1,2:T(8,128)(2,1)} copy(bf16[32,8,4096]{2,1,0:T(8,128)(2,1)S(1)} %constant_dynamic-update-slice_fusion) | data formatting | bytes 4194304 | tf_op jit(solution)/shard_map/concatenate | solution.py:58
  18.6 10.5 %slice.49 = f32[32,8,4080]{0,1,2:T(8,128)} slice(bf16[32,8,4096]{0,1,2:T(8,128)(2,1)} %copy.34), slice={[0:32], [0:8], [0:4080]} | slice | bytes 8355840 | tf_op jit(solution)/shard_map/slice | solution.py:24
  30.5 6.0 slice.50
  36.5 6.0 slice.51
  42.5 23.1 %fusion.44 = bf16[4096,8,32]{2,1,0:T(8,128)(2,1)} fusion(f32[32,8,4048]{0,1,2:T(8,128)} %slice.51, f32[8]{0:T(128)S(1)} %get-tuple-element.488, f32[32,8,4064]{0,1,2:T(8,128)} %slice.50, f32[8]{0:T(128)S(1)} %get-tuple-element.489, f32[32,8,4080]{0,1,2:T(8,128)} %slice.49, f32[8]{0:T(128)S(1)} %get-tuple-element.490, bf16[32,8,4096]{0,1,2:T(8,128)(2,1)} %copy.34, ...), kind=kLoop, calls=%fused_computation.88 | loop fusion | flops 9437184 | bytes 16679040
  65.6 14.5 %reshape.59 = bf16[16,2,32768]{2,1,0:T(2,128)(2,1)} reshape(bf16[4096,8,32]{2,1,0:T(8,128)(2,1)} %fusion.44) | data formatting | bytes 4194304
  80.1 11.3 %all-to-all-start = ((bf16[16,2,32768]{2,1,0:T(2,128)(2,1)}), bf16[16,2,32768]{2,1,0:T(2,128)(2,1)}, u32[]{:S(2)}, u32[]{:S(2)}) async-start(bf16[16,2,32768]{2,1,0:T(2,128)(2,1)} %reshape.59), calls=%async_computation | async-start | bytes 4194304 | tf_op jit(solution)/shard_map/all_to_all | solution.py:69
  91.4 50.5 %all-to-all-done = bf16[16,2,32768]{2,1,0:T(2,128)(2,1)} async-done(((bf16[16,2,32768]{2,1,0:T(2,128)(2,1)}), bf16[16,2,32768]{2,1,0:T(2,128)(2,1)}, u32[]{:S(2)}, u32[]{:S(2)}) %all-to-all-start) | async-done | bytes 2097184 | tf_op jit(solution)/shard_map/all_to_all | solution.py:69
  141.9 12.9 %reshape.60 = bf16[4096,8,32]{2,1,0:T(8,128)(2,1)} reshape(bf16[16,2,32768]{2,1,0:T(2,128)(2,1)} %all-to-all-done) | data formatting | bytes 4194304
  154.8 10.5 %copy.36 = bf16[32,16,8,256]{3,2,1,0:T(8,128)(2,1)} copy(bf16[32,16,8,256]{0,2,3,1:T(8,128)(2,1)} %bitcast.123) | data formatting | bytes 4194304 | tf_op jit(solution)/shard_map/all_to_all | solution.py:69
  165.3 6.2 fusion.12
  171.5 74.3 %psum.21 = bf16[32,256]{1,0:T(8,128)(2,1)S(1)} all-reduce(f32[32,256]{1,0:T(8,128)S(1)} %broadcast_multiply_fusion), channel_id=1, replica_groups=mesh['dp'=16,'chan'=16] {'chan'}, use_global_device_ids=true, to_apply=%region_1.2 | all-reduce | flops 8192 | bytes 49152 | tf_op jit(solution)/shard_map/psum | solution.py:73
  246.3 74.0 %while.40 = (s32[]{:T(128)}, bf16[16,1024]{1,0:T(8,128)(2,1)S(1)}, f32[16]{0:T(128)S(1)}, f32[16]{0:T(128)S(1)}, bf16[16,1024]{1,0:T(8,128)(2,1)S(1)}, /*index=5...) while((s32[]{:T(128)}, bf16[16,1024]{1,0:T(8,128)(2,1)S(1)}, ...), condition=%wide.region_6.7_spmd.clone, body=%wide.region_3.6_spmd.clone.sunk | while | flops 525888 | bytes 263144 | solution.py:97
  260.4 5.3 collective-permute-done
  265.9 5.3 collective-permute-done
  271.3 5.3 collective-permute-done
  282.2 5.3 collective-permute-done
  287.7 5.3 collective-permute-done
  293.2 5.3 collective-permute-done
  320.9 92.6 %while.41 = (s32[]{:T(128)}, bf16[16,1024]{1,0:T(8,128)(2,1)S(1)}, f32[16,1024]{1,0:T(8,128)S(1)}, f32[16,1024]{1,0:T(8,128)S(1)}, bf16[16,1024]{1,0:T(8,128)(2,...) while((s32[]{:T(128)}, bf16[16,1024]{1,0:T(8,128)(2,1)S(1)}, ...), condition=%wide.region_10.11_spmd.clone, body=%wide.region_9.10_spmd.clone.sunk | while | flops 1656608 | bytes 854104 | solution.py:126
  414.2 5.6 collective-permute-done.3
  445.1 64.7 %reduce-scatter.4.cloned.1.call-done = f32[64,16]{1,0:T(8,128)} async-done(((f32[1024,16]{1,0:T(8,128)}), f32[64,16]{1,0:T(8,128)}) %reduce-scatter.4.cloned.1.call-update) | async-done | bytes 4112
  516.8 28.9 %psum.22 = f32[8,4]{0,1:T(4,128)} all-reduce(f32[8,4]{0,1:T(4,128)S(1)} %pad_maximum_fusion.1), channel_id=1, replica_groups=mesh['dp'=16,'chan'=16] {'dp'}, use_global_device_ids=true, to_apply=%region_12.13 | all-reduce | flops 32 | bytes 256 | tf_op jit(solution)/shard_map/psum | solution.py:157
  545.7 153.7 %all-reduce.6.cloned.1.call-done = f32[256,128]{1,0:T(8,128)} async-done(((f32[256,128]{1,0:T(8,128)}), f32[256,128]{1,0:T(8,128)}) %all-reduce.6.cloned.1.call-update) | async-done | bytes 131088 | tf_op jit(solution)/shard_map/psum | solution.py:153
  (272 shorter events, 174.2 us)
Async XLA Ops:
  80.1 61.8 %all-to-all-start = ((bf16[16,2,32768]{2,1,0:T(2,128)(2,1)}), bf16[16,2,32768]{2,1,0:T(2,128)(2,1)}, u32[]{:S(2)}, u32[]{:S(2)}) async-start(bf16[16,2,32768]{2,1,0:T(2,128)(2,1)} %reshape.59), calls=%async_computation | async-start | bytes 4194304 | tf_op jit(solution)/shard_map/all_to_all | solution.py:69
  260.2 5.4 collective-permute-start
  265.7 5.4 collective-permute-start
  271.2 5.4 collective-permute-start
  320.9 5.5 collective-permute-start.1
  321.4 5.9 collective-permute-start.2
  327.6 5.6 collective-permute-start.2
  333.4 5.9 collective-permute-start.2
  339.6 5.9 collective-permute-start.2
  345.8 5.9 collective-permute-start.2
  352.0 5.9 collective-permute-start.2
  358.2 5.9 collective-permute-start.2
  364.4 5.9 collective-permute-start.2
  370.5 5.9 collective-permute-start.2
  376.7 5.9 collective-permute-start.2
  382.9 5.9 collective-permute-start.2
  389.1 5.9 collective-permute-start.2
  395.3 5.9 collective-permute-start.2
  401.5 5.9 collective-permute-start.2
  407.7 5.9 collective-permute-start.2
  413.8 6.1 collective-permute-start.3
  434.6 76.7 %all-to-all-start.1 = ((bf16[32,128,256]{2,0,1:T(8,128)(2,1)}), bf16[32,128,256]{2,0,1:T(8,128)(2,1)}, u32[]{:S(2)}, u32[]{:S(2)}) async-start(bf16[32,128,256]{2,0,1:T(8,128)(2,1)} %copy.39), calls=%async_computation.1 | async-start | bytes 4194304 | tf_op jit(solution)/shard_map/all_to_all | solution.py:154
  439.0 70.8 %reduce-scatter.4.cloned.1.call-start = ((), (), s32[]{:S(2)}) async-start(), calls=%async_computation.4 | async-start | bytes 557056
  440.2 259.2 %all-reduce.6.cloned.1.call-start = ((), (), s32[]{:S(2)}) async-start(), calls=%async_computation.3 | async-start | bytes 262144 | tf_op jit(solution)/shard_map/psum | solution.py:153
  (32 other events, 546.0 us)
Sparse Core Ops, SparseCore 0:
  442.3 67.4 reduce-scatter.3
Sparse Core Ops, SparseCore 1:
  446.8 252.6 all-reduce.5
where the time goes:
time: 710 us; the launch traced here: 708 us
  waiting for transfers between devices  403 us (57%)
  blocking collectives  103 us (15%)
  local copies, waits for them, and re-layouts  84.8 us (12%)
  starting transfers between devices  43.8 us (6%)
  other arithmetic  32.1 us (5%)
  matrix products  24.8 us (3%)
  between operations  15.7 us (2%)
    psum x1, waiting for transfers between devices, body(): grad_pw = lax.psum(mix_terms, ('dp', 'chan'))  154 us
    ppermute x46, waiting for transfers between devices, passed_along(): return lax.ppermute(value, axis, pairs)  135 us
    psum x1, blocking collectives, body(): pooled = lax.psum(partial_pool, 'chan')  74.3 us
    unnamed x3, waiting for transfers between devices  64.7 us
    all_to_all x1, waiting for transfers between devices, body(): lax.all_to_all(conv_local, 'chan', split_axis=2, concat_axis=1, tiled=True)  50.5 us
    unnamed x18, local copies, waits for them, and re-layouts  35.1 us
    psum x1, blocking collectives, body(): grad_dw = lax.psum(kernel_part, 'dp')  28.9 us
    ppermute x46, starting transfers between devices, passed_along(): return lax.ppermute(value, axis, pairs)  28.1 us
  transfers between devices with their start and end apart: 50, of which 49 were waited for; matrix products, arithmetic and copies ran while one was open for 3% of the time, Pallas kernels for 0%

commit v1 on v0

--- a/solution.py
+++ b/solution.py
@@ -66,7 +66,12 @@
     local_metrics = anchors.shape[1]
     local_kernel = lax.dynamic_slice_in_dim(dw_weight, chan_index * local_metrics, local_metrics, 0)
     conv_local = depthwise(stacked, local_kernel)
-    conv_rows = lax.all_to_all(conv_local, "chan", split_axis=2, concat_axis=1, tiled=True)
+    conv_rows = jnp.concatenate(
+        lax.all_to_all(
+            jnp.stack(jnp.split(conv_local, lax.axis_size("chan"), axis=2)), "chan", 0, 0
+        ),
+        axis=1,
+    )
     mixed = jnp.einsum("fc,nct->nft", pw_weight, conv_rows, preferred_element_type=jnp.float32)
     partial_pool = jnp.sum(jax.nn.silu(mixed), 2) / length
     conv_time, mixed, partial_pool = (conv_rows, mixed, partial_pool)

time: 710 us -> 640 us (0.901)
  local copies, waits for them, and re-layouts: 84.8 us -> 32.2 us
  other arithmetic: 32.1 us -> 15.4 us
    unnamed x4 -> x3, other arithmetic: 23.1 us -> 0.01 us
    unnamed x18 -> x31, local copies, waits for them, and re-layouts: 35.1 us -> 16.5 us
    slice x3, local copies, waits for them, and re-layouts: 22.4 us -> 7.36 us  [depthwise(): widened[:, :, :length - offset_steps]]
    all_to_all x1 -> x0, local copies, waits for them, and re-layouts: 10.5 us -> none  [body(): lax.all_to_all(conv_local, 'chan', split_axis=2, concat_axis=1, tiled=True)]
    concatenate x2 -> x1, local copies, waits for them, and re-layouts: 9.23 us -> 0.07 us  [body(): stacked = jnp.concatenate([anchors, views], 0)]
where the time goes in v1:
time: 640 us; the launch traced here: 639 us
  waiting for transfers between devices  404 us (63%)
  blocking collectives  103 us (16%)
  starting transfers between devices  44 us (7%)
  local copies, waits for them, and re-layouts  32.2 us (5%)
  matrix products  24.9 us (4%)
  between operations  15.7 us (2%)
  other arithmetic  15.4 us (2%)
    psum x1, waiting for transfers between devices, body(): grad_pw = lax.psum(mix_terms, ('dp', 'chan'))  154 us
    ppermute x46, waiting for transfers between devices, passed_along(): return lax.ppermute(value, axis, pairs)  135 us
    psum x1, blocking collectives, body(): pooled = lax.psum(partial_pool, 'chan')  74.3 us
    unnamed x3, waiting for transfers between devices  64.7 us
    all_to_all x1, waiting for transfers between devices, body(): lax.all_to_all(jnp.stack(jnp.split(conv_local, lax.axis_size('chan'), axi...  50.5 us
    psum x1, blocking collectives, body(): grad_dw = lax.psum(kernel_part, 'dp')  28.9 us
    ppermute x46, starting transfers between devices, passed_along(): return lax.ppermute(value, axis, pairs)  28.1 us
    unnamed x31, local copies, waits for them, and re-layouts  16.5 us
  transfers between devices with their start and end apart: 50, of which 49 were waited for; matrix products, arithmetic and copies ran while one was open for 3% of the time, Pallas kernels for 0%

profile of v1, /device:TPU:2, one launch (start us, length us, event | category | flops | bytes accessed | tf_op | source)
XLA Modules:
  0.0 639.4 jit_solution(2513624307807100844)
XLA Ops:
  17.1 6.4 add_convert_fusion
  34.2 11.4 %all-to-all-start = ((bf16[16,32,8,256]{3,2,1,0:T(8,128)(2,1)}), bf16[16,32,8,256]{3,2,1,0:T(8,128)(2,1)}, u32[]{:S(2)}, u32[]{:S(2)}) async-start(bf16[16,32,8,256]{3,2,1,0:T(8,128)(2,1)} %fusion.37), calls=%async_computation | async-start | bytes 4194304 | tf_op jit(solution)/shard_map/all_to_all | solution.py:70
  45.7 50.5 %all-to-all-done = bf16[16,32,8,256]{3,2,1,0:T(8,128)(2,1)} async-done(((bf16[16,32,8,256]{3,2,1,0:T(8,128)(2,1)}), bf16[16,32,8,256]{3,2,1,0:T(8,128)(2,1)}, u32[]{:S(2)}, u32[]{:S(2)}) %all-to-all-start) | async-done | bytes 2097184 | tf_op jit(solution)/shard_map/all_to_all | solution.py:70
  96.1 6.2 fusion.12
  102.3 74.3 %psum.21 = bf16[32,256]{1,0:T(8,128)(2,1)S(1)} all-reduce(f32[32,256]{1,0:T(8,128)S(1)} %broadcast_multiply_fusion), channel_id=1, replica_groups=mesh['dp'=16,'chan'=16] {'chan'}, use_global_device_ids=true, to_apply=%region_1.2 | all-reduce | flops 8192 | bytes 49152 | tf_op jit(solution)/shard_map/psum | solution.py:78
  177.1 74.0 %while.40 = (s32[]{:T(128)}, bf16[16,1024]{1,0:T(8,128)(2,1)S(1)}, f32[16]{0:T(128)S(1)}, f32[16]{0:T(128)S(1)}, bf16[16,1024]{1,0:T(8,128)(2,1)S(1)}, /*index=5...) while((s32[]{:T(128)}, bf16[16,1024]{1,0:T(8,128)(2,1)S(1)}, ...), condition=%wide.region_6.7_spmd.clone, body=%wide.region_3.6_spmd.clone.sunk | while | flops 525888 | bytes 263144 | solution.py:102
  191.3 5.3 collective-permute-done
  196.7 5.3 collective-permute-done
  202.2 5.3 collective-permute-done
  207.6 5.3 collective-permute-done
  213.1 5.3 collective-permute-done
  218.5 5.3 collective-permute-done
  224.0 5.3 collective-permute-done
  229.4 5.3 collective-permute-done
  234.9 5.3 collective-permute-done
  240.3 5.3 collective-permute-done
  245.8 5.3 collective-permute-done
  251.8 92.6 %while.41 = (s32[]{:T(128)}, bf16[16,1024]{1,0:T(8,128)(2,1)S(1)}, f32[16,1024]{1,0:T(8,128)S(1)}, f32[16,1024]{1,0:T(8,128)S(1)}, bf16[16,1024]{1,0:T(8,128)(2,...) while((s32[]{:T(128)}, bf16[16,1024]{1,0:T(8,128)(2,1)S(1)}, ...), condition=%wide.region_10.11_spmd.clone, body=%wide.region_9.10_spmd.clone.sunk | while | flops 1656608 | bytes 854104 | solution.py:131
  252.4 4.9 collective-permute-done.1
  345.1 5.6 collective-permute-done.3
  351.2 5.0 fusion.16
  375.9 64.7 %reduce-scatter.4.cloned.1.call-done = f32[64,16]{1,0:T(8,128)} async-done(((f32[1024,16]{1,0:T(8,128)}), f32[64,16]{1,0:T(8,128)}) %reduce-scatter.4.cloned.1.call-update) | async-done | bytes 4112
  447.6 28.9 %psum.22 = f32[8,4]{0,1:T(4,128)} all-reduce(f32[8,4]{0,1:T(4,128)S(1)} %pad_maximum_fusion.1), channel_id=1, replica_groups=mesh['dp'=16,'chan'=16] {'dp'}, use_global_device_ids=true, to_apply=%region_12.13 | all-reduce | flops 32 | bytes 256 | tf_op jit(solution)/shard_map/psum | solution.py:162
  476.5 153.8 %all-reduce.6.cloned.1.call-done = f32[256,128]{1,0:T(8,128)} async-done(((f32[256,128]{1,0:T(8,128)}), f32[256,128]{1,0:T(8,128)}) %all-reduce.6.cloned.1.call-update) | async-done | bytes 131088 | tf_op jit(solution)/shard_map/psum | solution.py:158
  (284 shorter events, 153.5 us)
Async XLA Ops:
  34.2 61.9 %all-to-all-start = ((bf16[16,32,8,256]{3,2,1,0:T(8,128)(2,1)}), bf16[16,32,8,256]{3,2,1,0:T(8,128)(2,1)}, u32[]{:S(2)}, u32[]{:S(2)}) async-start(bf16[16,32,8,256]{3,2,1,0:T(8,128)(2,1)} %fusion.37), calls=%async_computation | async-start | bytes 4194304 | tf_op jit(solution)/shard_map/all_to_all | solution.py:70
  191.1 5.4 collective-permute-start
  202.0 5.4 collective-permute-start
  207.4 5.4 collective-permute-start
  251.8 5.5 collective-permute-start.1
  252.2 5.9 collective-permute-start.2
  258.4 5.6 collective-permute-start.2
  264.3 5.9 collective-permute-start.2
  270.4 5.9 collective-permute-start.2
  276.6 5.9 collective-permute-start.2
  282.8 5.9 collective-permute-start.2
  289.0 5.9 collective-permute-start.2
  295.2 5.9 collective-permute-start.2
  301.4 5.9 collective-permute-start.2
  307.6 5.9 collective-permute-start.2
  313.7 5.9 collective-permute-start.2
  319.9 5.9 collective-permute-start.2
  326.1 5.9 collective-permute-start.2
  332.3 5.9 collective-permute-start.2
  338.5 5.9 collective-permute-start.2
  344.6 6.1 collective-permute-start.3
  365.4 76.6 %all-to-all-start.1 = ((bf16[32,128,256]{2,0,1:T(8,128)(2,1)}), bf16[32,128,256]{2,0,1:T(8,128)(2,1)}, u32[]{:S(2)}, u32[]{:S(2)}) async-start(bf16[32,128,256]{2,0,1:T(8,128)(2,1)} %copy.36), calls=%async_computation.1 | async-start | bytes 4194304 | tf_op jit(solution)/shard_map/all_to_all | solution.py:159
  369.8 70.8 %reduce-scatter.4.cloned.1.call-start = ((), (), s32[]{:S(2)}) async-start(), calls=%async_computation.4 | async-start | bytes 557056
  371.0 259.3 %all-reduce.6.cloned.1.call-start = ((), (), s32[]{:S(2)}) async-start(), calls=%async_computation.3 | async-start | bytes 262144 | tf_op jit(solution)/shard_map/psum | solution.py:158
  (32 other events, 501.5 us)
Sparse Core Ops, SparseCore 0:
  373.2 67.3 reduce-scatter.3
Sparse Core Ops, SparseCore 1:
  377.6 252.7 all-reduce.5
